TPU v7x, 128 devices: a whole 4x4x4 slice. The times are simulated.
128 devices in a mesh: basis: 64 (over z, y, x), ex: 2 (over core).
Axes of the slice: x: 4, y: 4, z: 4, core: 2. Of those that a mesh axis runs over, the one named last changes fastest.
Arguments:
- activations: bfloat16 [256, 768, 2880], P(('basis', 'ex')), may hold values from -6 to 6
- out_grads: bfloat16 [256, 768, 2880], P(('basis', 'ex')), may hold values from -0.25 to 0.25
- grad_basis: bfloat16 [2880, 256], replicated, may hold values from -0.109375 to 0.109375
- panel_store: bfloat16 [64, 4, 2880, 128], P('basis', None, 'ex'), may hold values from -0.109375 to 0.109375
- owners: int32 [4], replicated, may hold values from 0 to 63, as said below
- token_count: int32 [256], P(('basis', 'ex')), may hold values from 96 to 768, as said below
Outputs:
- scaled: float32 [256, 256, 512], P('basis', 'ex')
Inputs may be any that keep to these rules, and one draw needn't show every extreme that they name: `owners`: values are basis indices; panels may share an owner. `token_count`: some example has all 768 tokens live.
All inputs are finite; a program needn't handle non-finite values.
Results may differ from a plain program's by a relative error of at most 0.00045.
The roundings to bfloat16 on the way count: a program that leaves them out, or rounds other values in their place, can miss the bound.
Values may be sent and summed in bfloat16 or wider, within the bound.
No kernel may reach another device: no remote copies, remote signals or barrier semaphores. Data moves between devices by JAX's collectives and lax.ppermute only.
A program may use at most 128 MiB of HBM per device.

v0:
```python
import functools

import jax
import jax.numpy as jnp
from jax import lax
from jax.experimental import pallas as pl
from jax.experimental.pallas import tpu as pltpu
from jax.sharding import PartitionSpec as P

ROWS = 96
TT = 256
F32 = jnp.float32
BF16 = jnp.bfloat16


def grads_kernel(e_ref, act_ref, rg_ref, mine_ref, other_ref, keep_ref, send_ref, sq_ref, basis, acc, sq, sems):
    n, t = pl.program_id(0), pl.program_id(1)
    nt = pl.num_programs(1)
    e = e_ref[0]
    half = basis.shape[0] // 2
    panels = basis.shape[1] // 128

    def copies():
        out = []
        for h, src in enumerate((mine_ref, other_ref)):
            at = pl.multiple_of((e if h == 0 else 1 - e) * half, 16)
            for k in range(panels):
                out.append(
                    pltpu.make_async_copy(
                        src.at[pl.ds(k * half, half), :],
                        basis.at[pl.ds(at, half), pl.ds(k * 128, 128)],
                        sems.at[h * panels + k],
                    )
                )
        return out

    @pl.when((n == 0) & (t == 0))
    def _():
        for c in copies():
            c.start()
        for c in copies():
            c.wait()
        sq[...] = jnp.zeros_like(sq)

    rot = jnp.dot(act_ref[0], basis[...], preferred_element_type=F32).astype(BF16)
    part = jnp.dot(rg_ref[0], rot, preferred_element_type=F32)

    @pl.when(t == 0)
    def _():
        acc[...] = part

    @pl.when(t > 0)
    def _():
        acc[...] += part

    @pl.when(t == nt - 1)
    def _():
        dirs = acc.shape[0] // 2
        keep_ref[0] = acc[pl.ds(pl.multiple_of(e * dirs, 8), dirs), :]
        send_ref[0] = acc[pl.ds(pl.multiple_of((1 - e) * dirs, 8), dirs), :]
        sq[...] += acc[...] * acc[...]

    @pl.when((t == nt - 1) & (n == pl.num_programs(0) - 1))
    def _():
        dirs = acc.shape[0] // 2
        cols = acc.shape[1] // 128
        for h in range(2):
            for r in range(dirs // 8):
                for c in range(cols):
                    sq_ref[2 * (cols * r + c) + h] = sq[pl.ds(h * dirs + 8 * r, 8), pl.ds(128 * c, 128)]


def ex_gradients(e, act, rg, mine, other):
    local, tok, width = act.shape
    dirs = rg.shape[1]
    half = width // 2
    cols = mine.shape[0] // half * 128
    grid = (local, tok // TT)
    return pl.pallas_call(
        grads_kernel,
        grid_spec=pltpu.PrefetchScalarGridSpec(
            num_scalar_prefetch=1,
            grid=grid,
            in_specs=[
                pl.BlockSpec((1, TT, width), lambda n, t, e: (n, t, 0)),
                pl.BlockSpec((1, dirs, TT), lambda n, t, e: (n, 0, t)),
                pl.BlockSpec(memory_space=pl.ANY),
                pl.BlockSpec(memory_space=pl.ANY),
            ],
            out_specs=[
                pl.BlockSpec((1, dirs // 2, cols), lambda n, t, e: (n, 0, 0)),
                pl.BlockSpec((1, dirs // 2, cols), lambda n, t, e: (n, 0, 0)),
                pl.BlockSpec((dirs * cols // 1024, 8, 128), lambda n, t, e: (0, 0, 0)),
            ],
            scratch_shapes=[
                pltpu.VMEM((width, cols), BF16),
                pltpu.VMEM((dirs, cols), F32),
                pltpu.VMEM((dirs, cols), F32),
                pltpu.SemaphoreType.DMA((2 * (cols // 128),)),
            ],
        ),
        out_shape=[
            jax.ShapeDtypeStruct((local, dirs // 2, cols), F32),
            jax.ShapeDtypeStruct((local, dirs // 2, cols), F32),
            jax.ShapeDtypeStruct((dirs * cols // 1024, 8, 128), F32),
        ],
        compiler_params=pltpu.CompilerParams(vmem_limit_bytes=40 << 20),
    )(e, act, rg, mine, other)


def lambda_kernel(scale, x_ref, o_ref):
    lam = jnp.sum(x_ref[...], axis=0) * scale
    o_ref[...] = jnp.broadcast_to(lam[None], o_ref.shape)


def scale_kernel(e_ref, lam_ref, keep_ref, got_ref, o_ref):
    e = e_ref[0]
    local, dirs, cols = keep_ref.shape
    tiles = lam_ref.shape[0] // 2
    damp = jnp.sum(jnp.sum(lam_ref[...], axis=0), keepdims=True) * (0.1 / (lam_ref.size))
    across = cols // 128
    for i in range(tiles):
        r, c = i // across, i % across
        at = (slice(8 * r, 8 * r + 8), slice(128 * c, 128 * c + 128))
        inv = 1.0 / (lam_ref[2 * i + e] + damp)
        for j in range(local):
            o_ref[e * local + j, at[0], at[1]] = keep_ref[j, at[0], at[1]] * inv
            o_ref[(1 - e) * local + j, at[0], at[1]] = got_ref[j, at[0], at[1]] * inv


def per_device(activations, out_grads, grad_basis, panel_store, owners, token_count):
    local, tok, width = activations.shape
    _, panels, half, pw = panel_store.shape
    n_basis, n_ex = lax.axis_size("basis"), lax.axis_size("ex")
    b, e = lax.axis_index("basis"), lax.axis_index("ex")
    both = ("basis", "ex")
    e1 = e.reshape(1).astype(jnp.int32)

    blocks = half // ROWS
    slots = panel_store.reshape(panels * blocks, ROWS, pw)
    spare = n_basis - panels * blocks
    slots = jnp.concatenate([slots, slots[:spare]], axis=0)
    arrived = lax.all_to_all(slots, "basis", 0, 0, tiled=True)
    owner = owners[jnp.minimum(b // blocks, panels - 1)]
    block = lax.dynamic_index_in_dim(arrived, owner, 0, keepdims=True)
    spread = jnp.broadcast_to(block, arrived.shape)
    mine = lax.all_to_all(spread, "basis", 0, 0, tiled=True).reshape(n_basis * ROWS, pw)
    swap = [(0, 1), (1, 0)]
    other = lax.ppermute(mine, "ex", swap)

    rg = lax.dot_general(grad_basis, out_grads, (((0,), (2,)), ((), ())), preferred_element_type=F32)
    rg = jnp.transpose(rg, (1, 0, 2)).astype(BF16)
    live = jnp.arange(tok)[None, :] < token_count[:, None]
    rg = jnp.where(live[:, None, :], rg, jnp.zeros((), BF16))

    keep, send, squares = ex_gradients(e1, activations, rg, mine, other)
    got = lax.ppermute(send, "ex", swap)
    ex_count = local * n_basis * n_ex
    parts = lax.all_to_all(squares, both, 0, 0, tiled=True)
    lam = pl.pallas_call(
        functools.partial(lambda_kernel, 1.0 / ex_count),
        out_shape=jax.ShapeDtypeStruct(parts.shape, F32),
    )(parts)
    lam = lax.all_to_all(lam, both, 0, 0, tiled=True)
    return pl.pallas_call(
        scale_kernel,
        in_specs=[pl.BlockSpec(memory_space=pltpu.SMEM)] + [pl.BlockSpec(memory_space=pltpu.VMEM)] * 3,
        out_shape=jax.ShapeDtypeStruct((2 * local, keep.shape[1], keep.shape[2]), F32),
    )(e1, lam, keep, got)


def solution(mesh):
    return jax.shard_map(
        per_device,
        mesh=mesh,
        in_specs=(
            P(("basis", "ex"), None, None),
            P(("basis", "ex"), None, None),
            P(),
            P("basis", None, "ex", None),
            P(),
            P(("basis", "ex")),
        ),
        out_specs=P("basis", "ex", None),
        check_vma=False,
    )
```

profile of v0, /device:TPU:1, one launch (start us, length us, event | category | flops | bytes accessed | tf_op | source)
XLA Modules:
  0.0 142.1 jit_solution(10944550457549349963)
XLA Ops:
  0.0 0.0 copy-start
  0.0 1.0 slice.4
  1.0 2.7 %pad_maximum_fusion = bf16[64,96,128]{2,1,0:T(8,128)(2,1)} fusion(bf16[4,96,128]{2,1,0:T(8,128)(2,1)S(1)} %slice.4, bf16[60,96,128]{2,1,0:T(8,128)(2,1)} %bitcast.21), kind=kLoop, calls=%fused_computation | loop fusion | flops 786432 | bytes 3145728 | tf_op jit(solution)/shard_map/concatenate | solution.py:142
  3.7 12.1 %all-to-all-start = ((bf16[64,96,128]{2,1,0:T(8,128)(2,1)}), bf16[64,96,128]{2,1,0:T(8,128)(2,1)S(1)}, u32[]{:S(2)}, u32[]{:S(2)}) async-start(bf16[64,96,128]{2,1,0:T(8,128)(2,1)} %pad_maximum_fusion), calls=%async_computation | async-start | bytes 3145728 | tf_op jit(solution)/shard_map/all_to_all | solution.py:143
  15.8 0.0 copy-done.9
  15.8 0.6 dynamic_slice.7
  18.4 20.4 %all-to-all-done = bf16[64,96,128]{2,1,0:T(8,128)(2,1)S(1)} async-done(((bf16[64,96,128]{2,1,0:T(8,128)(2,1)}), bf16[64,96,128]{2,1,0:T(8,128)(2,1)S(1)}, u32[]{:S(2)}, u32[]{:S(2)}) %all-to-all-start) | async-done | bytes 1572896 | tf_op jit(solution)/shard_map/all_to_all | solution.py:143
  38.8 0.2 broadcast_in_dim.25
  39.0 27.1 %all_to_all.20 = bf16[64,96,128]{2,1,0:T(8,128)(2,1)S(1)} all-to-all(bf16[64,96,128]{2,1,0:T(8,128)(2,1)S(1)} %broadcast_in_dim.25), channel_id=1, replica_groups=mesh['basis'=64,'ex'=2] {'basis'}, dimensions={0} | all-to-all | bytes 3145728 | tf_op jit(solution)/shard_map/all_to_all | solution.py:147
  66.2 3.3 %collective-permute-start = (bf16[6144,128]{1,0:T(8,128)(2,1)S(1)}, bf16[6144,128]{1,0:T(8,128)(2,1)}, u32[]{:S(2)}, u32[]{:S(2)}) collective-permute-start(bf16[6144,128]{1,0:T(8,128)(2,1)S(1)} %bitcast.18), channel_id=1, source_target_pairs={{0,1},{1,0},{2,3},{3,2},{4,5},{5,4},{6,7},{7,6},{8,9},{9,8},{10,11... | collective-permute-start | bytes 4718600 | tf_op jit(solution)/shard_map/ppermute | solution.py:149
  69.4 12.5 %copy.7.act_ref = bf16[2,768,2880]{2,1,0:T(8,128)(2,1)} copy(bf16[2,768,2880]{1,2,0:T(8,128)(2,1)} %param.6) | data formatting | bytes 17694720 | tf_op args[0]
  81.9 0.0 copy-done.8
  81.9 0.1 iota_compare_fusion
  82.0 0.0 copy-done
  82.0 6.3 %fusion.8.rg_ref = bf16[2,256,768]{2,1,0:T(8,128)(2,1)S(1)} fusion(bf16[2,768,2880]{1,2,0:T(8,128)(2,1)} %param.7, bf16[2880,256]{1,0:T(8,128)(2,1)S(1)} %copy-done, pred[2,768]{1,0:T(4,128)(4,1)S(1)} %iota_compare_fusion), kind=kOutput, calls=%fused_computation.5 | convolution fusion | flops 2265710592 | bytes 11109888 | tf_op jit(solution)/shard_map/dot_general | solution.py:151
  88.3 0.0 collective-permute-done.other_ref
  88.3 9.5 %shard_map.64 = (f32[2,128,512]{2,1,0:T(8,128)S(1)}, f32[2,128,512]{2,1,0:T(8,128)S(1)}, f32[128,8,128]{2,1,0:T(8,128)S(1)}) custom-call(s32[1]{0:T(128)} %bitcast.e_ref, bf16[2,768,2880]{2,1,0:T(8,128)(2,1)S(1)} %copy-done.1, bf16[2,256,768]{2,1,0:T(8,128)(2,1)S(1)} %fusion.8.rg_ref, bf16[6144,128]{1,0:T(8,128)(2,1)S(1)} %bitcast.19, ...), custom_call_target="tpu_custom_call" | custom-call | tf_op jit(solution)/shard_map/pallas_call | solution.py:79
  97.8 0.0 copy-start.2
  97.8 0.8 copy-done.2
  98.6 0.8 copy-done.3
  99.4 0.8 copy-done.4
  100.2 3.6 %all-to-all-start.2 = ((f32[128,8,128]{2,1,0:T(8,128)}), f32[128,8,128]{2,1,0:T(8,128)S(1)}, u32[]{:S(2)}, u32[]{:S(2)}) async-start(f32[128,8,128]{2,1,0:T(8,128)} %copy-done.2), calls=%async_computation.2 | async-start | bytes 1048576 | tf_op jit(solution)/shard_map/all_to_all | solution.py:159
  103.7 1.2 collective-permute-start.1
  104.9 12.6 %all-to-all-done.2.x_ref = f32[128,8,128]{2,1,0:T(8,128)S(1)} async-done(((f32[128,8,128]{2,1,0:T(8,128)}), f32[128,8,128]{2,1,0:T(8,128)S(1)}, u32[]{:S(2)}, u32[]{:S(2)}) %all-to-all-start.2) | async-done | bytes 524320 | tf_op jit(solution)/shard_map/all_to_all | solution.py:159
  117.5 0.8 copy-done.5
  118.3 2.0 %shard_map.65 = f32[128,8,128]{2,1,0:T(8,128)} custom-call(f32[128,8,128]{2,1,0:T(8,128)} %copy-done.5), custom_call_target="tpu_custom_call" | custom-call | tf_op jit(solution)/shard_map/pallas_call | solution.py:160
  120.3 4.5 %all-to-all-start.3 = ((f32[128,8,128]{2,1,0:T(8,128)}), f32[128,8,128]{2,1,0:T(8,128)S(1)}, u32[]{:S(2)}, u32[]{:S(2)}) async-start(f32[128,8,128]{2,1,0:T(8,128)} %shard_map.65), calls=%async_computation.3 | async-start | bytes 1048576 | tf_op jit(solution)/shard_map/all_to_all | solution.py:164
  124.8 0.0 collective-permute-done.1.got_ref
  124.8 0.0 copy-start.7
  124.8 13.7 %all-to-all-done.3.lam_ref = f32[128,8,128]{2,1,0:T(8,128)S(1)} async-done(((f32[128,8,128]{2,1,0:T(8,128)}), f32[128,8,128]{2,1,0:T(8,128)S(1)}, u32[]{:S(2)}, u32[]{:S(2)}) %all-to-all-start.3) | async-done | bytes 524320 | tf_op jit(solution)/shard_map/all_to_all | solution.py:164
  138.5 0.8 copy-done.6
  139.4 2.7 %shard_map.66 = f32[4,128,512]{2,1,0:T(8,128)} custom-call(s32[1]{0:T(128)} %bitcast.e_ref, f32[128,8,128]{2,1,0:T(8,128)} %copy-done.6, f32[2,128,512]{2,1,0:T(8,128)} %copy-done.3, f32[2,128,512]{2,1,0:T(8,128)} %copy-done.7), custom_call_target="tpu_custom_call" | custom-call | tf_op jit(solution)/shard_map/pallas_call | solution.py:165
  (10 shorter events, 0.0 us)
Async XLA Ops:
  0.0 82.0 %copy-start = (bf16[2880,256]{1,0:T(8,128)(2,1)S(1)}, bf16[2880,256]{1,0:T(8,128)(2,1)}, u32[]{:S(2)}) copy-start(bf16[2880,256]{1,0:T(8,128)(2,1)} %param.8) | copy-start | bytes 4423684
  3.7 12.1 %copy-start.9 = (s32[4]{0:T(128)S(1)}, s32[4]{0:T(128)}, u32[]{:S(2)}) copy-start(s32[4]{0:T(128)} %param.10) | copy-start | bytes 52
  3.7 35.1 %all-to-all-start = ((bf16[64,96,128]{2,1,0:T(8,128)(2,1)}), bf16[64,96,128]{2,1,0:T(8,128)(2,1)S(1)}, u32[]{:S(2)}, u32[]{:S(2)}) async-start(bf16[64,96,128]{2,1,0:T(8,128)(2,1)} %pad_maximum_fusion), calls=%async_computation | async-start | bytes 3145728 | tf_op jit(solution)/shard_map/all_to_all | solution.py:143
  66.2 22.1 %collective-permute-start = (bf16[6144,128]{1,0:T(8,128)(2,1)S(1)}, bf16[6144,128]{1,0:T(8,128)(2,1)}, u32[]{:S(2)}, u32[]{:S(2)}) collective-permute-start(bf16[6144,128]{1,0:T(8,128)(2,1)S(1)} %bitcast.18), channel_id=1, source_target_pairs={{0,1},{1,0},{2,3},{3,2},{4,5},{5,4},{6,7},{7,6},{8,9},{9,8},{10,11... | collective-permute-start | bytes 4718600 | tf_op jit(solution)/shard_map/ppermute | solution.py:149
  69.4 12.5 %copy-start.8 = (s32[2]{0:T(128)S(1)}, s32[2]{0:T(128)}, u32[]{:S(2)}) copy-start(s32[2]{0:T(128)} %param.11) | copy-start | bytes 28
  82.0 6.3 %copy-start.1 = (bf16[2,768,2880]{2,1,0:T(8,128)(2,1)S(1)}, bf16[2,768,2880]{2,1,0:T(8,128)(2,1)}, u32[]{:S(2)}) copy-start(bf16[2,768,2880]{2,1,0:T(8,128)(2,1)} %copy.7.act_ref) | copy-start | bytes 26542084
  97.8 0.8 copy-start.2
  98.5 0.8 copy-start.3
  99.4 0.8 copy-start.4
  100.2 17.3 %all-to-all-start.2 = ((f32[128,8,128]{2,1,0:T(8,128)}), f32[128,8,128]{2,1,0:T(8,128)S(1)}, u32[]{:S(2)}, u32[]{:S(2)}) async-start(f32[128,8,128]{2,1,0:T(8,128)} %copy-done.2), calls=%async_computation.2 | async-start | bytes 1048576 | tf_op jit(solution)/shard_map/all_to_all | solution.py:159
  103.7 21.1 %collective-permute-start.1 = (f32[2,128,512]{2,1,0:T(8,128)}, f32[2,128,512]{2,1,0:T(8,128)S(1)}, u32[]{:S(2)}, u32[]{:S(2)}) collective-permute-start(f32[2,128,512]{2,1,0:T(8,128)} %copy-done.4), channel_id=1, source_target_pairs={{0,1},{1,0},{2,3},{3,2},{4,5},{5,4},{6,7},{7,6},{8,9},{9,8},{10,11... | collective-permute-start | bytes 1572872 | tf_op jit(solution)/shard_map/ppermute | solution.py:157
  117.5 0.8 copy-start.5
  120.3 18.2 %all-to-all-start.3 = ((f32[128,8,128]{2,1,0:T(8,128)}), f32[128,8,128]{2,1,0:T(8,128)S(1)}, u32[]{:S(2)}, u32[]{:S(2)}) async-start(f32[128,8,128]{2,1,0:T(8,128)} %shard_map.65), calls=%async_computation.3 | async-start | bytes 1048576 | tf_op jit(solution)/shard_map/all_to_all | solution.py:164
  124.8 13.7 %copy-start.7 = (f32[2,128,512]{2,1,0:T(8,128)}, f32[2,128,512]{2,1,0:T(8,128)S(1)}, u32[]{:S(2)}) copy-start(f32[2,128,512]{2,1,0:T(8,128)S(1)} %collective-permute-done.1.got_ref) | copy-start | bytes 1572868
  138.5 0.8 copy-start.6
where the time goes:
time: 143 us; the launch traced here: 142 us
  waiting for transfers between devices  46.7 us (33%)
  blocking collectives  27.1 us (19%)
  starting transfers between devices  24.6 us (17%)
  local copies, waits for them, and re-layouts  18.3 us (13%)
  Pallas kernels  14.2 us (10%)
  matrix products  6.28 us (4%)
  other arithmetic  2.75 us (2%)
  between operations  2.08 us (1%)
    all_to_all x1, blocking collectives, per_device(): lax.all_to_all(spread, 'basis', 0, 0, tiled=True)  27.1 us
    all_to_all x1, waiting for transfers between devices, per_device(): arrived = lax.all_to_all(slots, 'basis', 0, 0, tiled=True)  20.4 us
    unnamed x21, local copies, waits for them, and re-layouts  16.5 us
    all_to_all x1, waiting for transfers between devices, per_device(): lam = lax.all_to_all(lam, both, 0, 0, tiled=True)  13.7 us
    all_to_all x1, waiting for transfers between devices, per_device(): parts = lax.all_to_all(squares, both, 0, 0, tiled=True)  12.6 us
    all_to_all x1, starting transfers between devices, per_device(): arrived = lax.all_to_all(slots, 'basis', 0, 0, tiled=True)  12.1 us
    pallas_call x1, Pallas kernels, ex_gradients(): pl.pallas_call(grads_kernel, grid_spec=pltpu.PrefetchScalarGridSpec(num_s...  9.46 us
    dot_general x1, matrix products, per_device(): lax.dot_general(grad_basis, out_grads, (((0,), (2,)), ((), ())), preferre...  6.28 us
  transfers between devices with their start and end apart: 5, of which 3 were waited for; matrix products, arithmetic and copies ran while one was open for 14% of the time, Pallas kernels for 1%

commit v1 on v0

v1 whole, which is shorter than its diff:
```python
import jax
import jax.numpy as jnp
from jax import lax
from jax.experimental import pallas as pl
from jax.experimental.pallas import tpu as pltpu
from jax.sharding import PartitionSpec as P

ROWS = 96
TT = 256
F32 = jnp.float32
BF16 = jnp.bfloat16


def turn_kernel(e_ref, x_ref, o_ref):
    o_ref[0, 0] = x_ref[0].T


def turned(e, activations):
    local, tok, width = activations.shape
    half = width // 2
    return pl.pallas_call(
        turn_kernel,
        grid_spec=pltpu.PrefetchScalarGridSpec(
            num_scalar_prefetch=1,
            grid=(2, local, tok // TT),
            in_specs=[pl.BlockSpec((1, half, TT), lambda h, n, t, e: (n, h + e[0] - 2 * h * e[0], t))],
            out_specs=pl.BlockSpec((1, 1, TT, half), lambda h, n, t, e: (h, n, t, 0)),
        ),
        out_shape=pltpu.HBM((2, local, tok, half), BF16),
        compiler_params=pltpu.CompilerParams(vmem_limit_bytes=24 << 20),
        cost_estimate=pl.CostEstimate(flops=0, transcendentals=0, bytes_accessed=4 * local * tok * width),
    )(e, pltpu.with_memory_space_constraint(jnp.swapaxes(activations, 1, 2), pltpu.HBM))


def half_product(act, basis_ref, half, p):
    pair = jnp.concatenate([basis_ref[pl.ds(k * half, half), :] for k in (p, p + 1)], axis=1)
    return jnp.dot(act, pair, preferred_element_type=F32)


def first_kernel(act_ref, basis_ref, o_ref):
    act = act_ref[0, 0]
    half = act.shape[1]
    for p in range(0, o_ref.shape[2] // 128, 2):
        o_ref[0, :, pl.ds(p * 128, 256)] = half_product(act, basis_ref, half, p)


def second_kernel(e_ref, act_ref, rg_ref, first_ref, basis_ref, keep_ref, send_ref, sq_ref, acc, sq):
    n, t = pl.program_id(0), pl.program_id(1)
    nt = pl.num_programs(1)
    e = e_ref[0]
    act = act_ref[0, 0]
    half = act.shape[1]
    for p in range(0, acc.shape[1] // 128, 2):
        at = pl.ds(p * 128, 256)
        rot = (first_ref[0, :, at] + half_product(act, basis_ref, half, p)).astype(BF16)
        part = jnp.dot(rg_ref[0], rot, preferred_element_type=F32)
        acc[:, at] = jnp.where(t == 0, part, acc[:, at] + part)

    @pl.when(t == nt - 1)
    def _():
        dirs = acc.shape[0] // 2
        keep_ref[0] = acc[pl.ds(pl.multiple_of(e * dirs, 8), dirs), :]
        send_ref[0] = acc[pl.ds(pl.multiple_of((1 - e) * dirs, 8), dirs), :]

    @pl.when((t == nt - 1) & (n == 0))
    def _():
        sq[...] = acc[...] * acc[...]

    @pl.when((t == nt - 1) & (n > 0))
    def _():
        sq[...] += acc[...] * acc[...]

    @pl.when((t == nt - 1) & (n == pl.num_programs(0) - 1))
    def _():
        dirs = acc.shape[0] // 2
        cols = acc.shape[1] // 128
        for h in range(2):
            for r in range(dirs // 8):
                for c in range(cols):
                    sq_ref[2 * (cols * r + c) + h] = sq[pl.ds(h * dirs + 8 * r, 8), pl.ds(128 * c, 128)]


def first_half(act, mine, panels):
    _, local, tok, half = act.shape
    cols = panels * 128
    return pl.pallas_call(
        first_kernel,
        grid=(local, tok // TT),
        in_specs=[
            pl.BlockSpec((1, 1, TT, half), lambda n, t: (0, n, t, 0)),
            pl.BlockSpec((panels * half, 128), lambda n, t: (0, 0)),
        ],
        out_specs=pl.BlockSpec((1, TT, cols), lambda n, t: (n, t, 0)),
        out_shape=jax.ShapeDtypeStruct((local, tok, cols), F32),
        compiler_params=pltpu.CompilerParams(vmem_limit_bytes=24 << 20),
        cost_estimate=pl.CostEstimate(
            flops=2 * local * tok * half * cols, transcendentals=0, bytes_accessed=2 * local * tok * half
        ),
    )(pltpu.with_memory_space_constraint(act, pltpu.HBM), mine)


def ex_gradients(e, act, rg, first, other):
    _, local, tok, half = act.shape
    dirs, cols = rg.shape[1], first.shape[2]
    panels = cols // 128
    return pl.pallas_call(
        second_kernel,
        grid_spec=pltpu.PrefetchScalarGridSpec(
            num_scalar_prefetch=1,
            grid=(local, tok // TT),
            in_specs=[
                pl.BlockSpec((1, 1, TT, half), lambda n, t, e: (1, n, t, 0)),
                pl.BlockSpec((1, dirs, TT), lambda n, t, e: (n, 0, t)),
                pl.BlockSpec((1, TT, cols), lambda n, t, e: (n, t, 0)),
                pl.BlockSpec((panels * half, 128), lambda n, t, e: (0, 0)),
            ],
            out_specs=[
                pl.BlockSpec((1, dirs // 2, cols), lambda n, t, e: (n, 0, 0)),
                pl.BlockSpec((1, dirs // 2, cols), lambda n, t, e: (n, 0, 0)),
                pl.BlockSpec((dirs * cols // 1024, 8, 128), lambda n, t, e: (0, 0, 0)),
            ],
            scratch_shapes=[pltpu.VMEM((dirs, cols), F32), pltpu.VMEM((dirs, cols), F32)],
        ),
        out_shape=[
            pltpu.HBM((local, dirs // 2, cols), F32),
            pltpu.HBM((local, dirs // 2, cols), F32),
            pltpu.HBM((dirs * cols // 1024, 8, 128), F32),
        ],
        compiler_params=pltpu.CompilerParams(vmem_limit_bytes=32 << 20),
        cost_estimate=pl.CostEstimate(
            flops=2 * local * tok * half * cols, transcendentals=0, bytes_accessed=2 * local * tok * half
        ),
    )(e, pltpu.with_memory_space_constraint(act, pltpu.HBM), rg, first, other)


def scale_kernel(e_ref, lam_ref, keep_ref, got_ref, o_ref, inv):
    e, i = e_ref[0], pl.program_id(0)
    local, dirs, cols = keep_ref.shape
    tiles, across = lam_ref.shape[0] // 2, cols // 128

    @pl.when(i == 0)
    def _():
        damp = jnp.sum(jnp.sum(lam_ref[...], axis=0), keepdims=True) * (0.1 / lam_ref.size)
        for j in range(tiles):
            r, c = j // across, j % across
            inv[pl.ds(8 * r, 8), pl.ds(128 * c, 128)] = 1.0 / (lam_ref[2 * j + e] + damp)

    for core in range(2):
        for j in range(local):
            for own in range(2):

                @pl.when((i == core * local + j) & (own == (e == core)))
                def _():
                    src = keep_ref if own else got_ref
                    o_ref[0] = src[j] * inv[...]


def scaled_rows(e, lam, keep, got):
    local, dirs, cols = keep.shape

    def whole(x):
        return pl.BlockSpec(x.shape, lambda i, e: (0, 0, 0))

    return pl.pallas_call(
        scale_kernel,
        grid_spec=pltpu.PrefetchScalarGridSpec(
            num_scalar_prefetch=1,
            grid=(2 * local,),
            in_specs=[whole(lam), whole(keep), whole(got)],
            out_specs=pl.BlockSpec((1, dirs, cols), lambda i, e: (i, 0, 0)),
            scratch_shapes=[pltpu.VMEM((dirs, cols), F32)],
        ),
        out_shape=jax.ShapeDtypeStruct((2 * local, dirs, cols), F32),
        compiler_params=pltpu.CompilerParams(vmem_limit_bytes=8 << 20),
    )(e, lam, keep, got)


def per_device(activations, out_grads, grad_basis, panel_store, owners, token_count):
    local, tok, width = activations.shape
    _, panels, half, pw = panel_store.shape
    n_basis, n_ex = lax.axis_size("basis"), lax.axis_size("ex")
    b, e = lax.axis_index("basis"), lax.axis_index("ex")
    both = ("basis", "ex")
    e1 = e.reshape(1).astype(jnp.int32)

    blocks = half // ROWS
    slots = panel_store.reshape(panels * blocks, ROWS, pw)
    slots = jnp.pad(slots, ((0, n_basis - panels * blocks), (0, 0), (0, 0)))
    arrived = lax.all_to_all(slots, "basis", 0, 0, tiled=True)
    act = turned(e1, activations)
    arrived, act = lax.optimization_barrier((arrived, act))

    owner = owners[jnp.minimum(b // blocks, panels - 1)]
    block = lax.dynamic_index_in_dim(arrived, owner, 0, keepdims=True)
    spread = jnp.broadcast_to(block, arrived.shape)
    mine = lax.all_to_all(spread, "basis", 0, 0, tiled=True)

    rg = lax.dot_general(grad_basis, out_grads, (((0,), (2,)), ((), ())), preferred_element_type=F32)
    rg = jnp.transpose(rg, (1, 0, 2)).astype(BF16)
    live = jnp.arange(tok)[None, :] < token_count[:, None]
    rg = jnp.where(live[:, None, :], rg, jnp.zeros((), BF16))
    mine, rg = lax.optimization_barrier((mine, rg))

    mine = mine.reshape(n_basis * ROWS, pw)
    swap = [(0, 1), (1, 0)]
    other = lax.ppermute(mine, "ex", swap)
    first = first_half(act, mine, panels)
    keep, send, squares = ex_gradients(e1, act, rg, first, other)
    got = lax.ppermute(send, "ex", swap)
    parts = lax.all_to_all(squares, both, 0, 0, tiled=True)
    lam = jnp.sum(parts, axis=0, keepdims=True) * (1.0 / (local * n_basis * n_ex))
    lam = lax.all_to_all(jnp.broadcast_to(lam, parts.shape), both, 0, 0, tiled=True)
    return scaled_rows(e1, lam, keep, got)


def solution(mesh):
    return jax.shard_map(
        per_device,
        mesh=mesh,
        in_specs=(
            P(("basis", "ex"), None, None),
            P(("basis", "ex"), None, None),
            P(),
            P("basis", None, "ex", None),
            P(),
            P(("basis", "ex")),
        ),
        out_specs=P("basis", "ex", None),
        check_vma=False,
    )
```

time: 143 us -> 127 us (0.89)
  blocking collectives: 27.1 us -> 0 us
  Pallas kernels: 14.2 us -> 31.5 us
  local copies, waits for them, and re-layouts: 18.3 us -> 5.56 us
  starting transfers between devices: 24.6 us -> 30.5 us
  waiting for transfers between devices: 46.7 us -> 49.7 us
  other arithmetic: 2.75 us -> 0.22 us
    all_to_all x1 -> x0, blocking collectives: 27.1 us -> none  [per_device(): lax.all_to_all(spread, 'basis', 0, 0, tiled=True)]
    pallas_call x3 -> x4, Pallas kernels: 14.2 us -> 31.5 us  [the longest x1 12.6 us: turned(): pl.pallas_call(turn_kernel, grid_spec=pltpu.PrefetchScalarGridSpec(num_sc...]
    unnamed x21 -> x8, local copies, waits for them, and re-layouts: 16.5 us -> 0.02 us
    all_to_all x1 -> x2, waiting for transfers between devices: 13.7 us -> 29.3 us  [the longest x1 15.6 us: per_device(): mine = lax.all_to_all(spread, 'basis', 0, 0, tiled=True)]
    all_to_all x1, waiting for transfers between devices: 20.4 us -> 7.85 us  [per_device(): arrived = lax.all_to_all(slots, 'basis', 0, 0, tiled=True)]
    all_to_all x1 -> x2, starting transfers between devices: 4.51 us -> 10.2 us  [the longest x1 5.65 us: per_device(): mine = lax.all_to_all(spread, 'basis', 0, 0, tiled=True)]
    pad x0 -> x1, local copies, waits for them, and re-layouts: none -> 2.75 us  [per_device(): slots = jnp.pad(slots, ((0, n_basis - panels * blocks), (0, 0), (0, 0)))]
    concatenate x1 -> x0, other arithmetic: 2.68 us -> none  [per_device(): slots = jnp.concatenate([slots, slots[:spare]], axis=0)]
  transfers between devices with their start and end apart: 5 -> 6, of which waited for: 3 -> 4; matrix products, arithmetic and copies ran while one was open for 14% -> 6% of each run, Pallas kernels for 1% -> 15%
where the time goes in v1:
time: 127 us; the launch traced here: 126 us
  waiting for transfers between devices  49.7 us (39%)
  Pallas kernels  31.5 us (25%)
  starting transfers between devices  30.5 us (24%)
  matrix products  6.12 us (5%)
  local copies, waits for them, and re-layouts  5.56 us (4%)
  between operations  2.07 us (2%)
    all_to_all x1, waiting for transfers between devices, per_device(): mine = lax.all_to_all(spread, 'basis', 0, 0, tiled=True)  15.6 us
    all_to_all x1, waiting for transfers between devices, per_device(): lax.all_to_all(jnp.broadcast_to(lam, parts.shape), both, 0, 0, tiled=True)  13.7 us
    pallas_call x1, Pallas kernels, turned(): pl.pallas_call(turn_kernel, grid_spec=pltpu.PrefetchScalarGridSpec(num_sc...  12.6 us
    all_to_all x1, waiting for transfers between devices, per_device(): parts = lax.all_to_all(squares, both, 0, 0, tiled=True)  12.6 us
    all_to_all x1, starting transfers between devices, per_device(): arrived = lax.all_to_all(slots, 'basis', 0, 0, tiled=True)  12.1 us
    pallas_call x1, Pallas kernels, ex_gradients(): pl.pallas_call(second_kernel, grid_spec=pltpu.PrefetchScalarGridSpec(num_...  10.6 us
    all_to_all x1, waiting for transfers between devices, per_device(): arrived = lax.all_to_all(slots, 'basis', 0, 0, tiled=True)  7.85 us
    pallas_call x1, Pallas kernels, first_half(): pl.pallas_call(first_kernel, grid=(local, tok // TT), in_specs=[pl.BlockS...  6.35 us
  transfers between devices with their start and end apart: 6, of which 4 were waited for; matrix products, arithmetic and copies ran while one was open for 6% of the time, Pallas kernels for 15%

profile of v1, /device:TPU:1, one launch (start us, length us, event | category | flops | bytes accessed | tf_op | source)
XLA Modules:
  0.0 125.7 jit_solution(5330406392820097856)
XLA Ops:
  0.0 0.0 copy-start
  0.0 2.7 %pad.4 = bf16[64,96,128]{2,1,0:T(8,128)(2,1)} pad(bf16[60,96,128]{2,1,0:T(8,128)(2,1)} %bitcast.20, bf16[]{:T(256)} %constant.11.clone.1), padding=0_4x0_0x0_0 | pad | bytes 3047426 | tf_op jit(solution)/shard_map/jit(_pad)/pad | solution.py:188
  2.8 0.0 copy-start.3
  2.8 12.1 %all-to-all-start = ((bf16[64,96,128]{2,1,0:T(8,128)(2,1)}), bf16[64,96,128]{2,1,0:T(8,128)(2,1)S(1)}, u32[]{:S(2)}, u32[]{:S(2)}) async-start(bf16[64,96,128]{2,1,0:T(8,128)(2,1)} %pad.4), calls=%async_computation | async-start | bytes 3145728 | tf_op jit(solution)/shard_map/all_to_all | solution.py:189
  14.9 0.0 copy-done.3
  14.9 0.6 dynamic_slice.7
  17.4 12.6 %shard_map.64.act_ref = bf16[2,2,768,1440]{3,2,1,0:T(8,128)(2,1)} custom-call(s32[1]{0:T(128)} %bitcast.e_ref, bf16[2,2880,768]{2,1,0:T(8,128)(2,1)} %bitcast.19), custom_call_target="tpu_custom_call" | custom-call | bytes 17694720 | tf_op jit(solution)/shard_map/pallas_call | solution.py:21
  30.0 7.8 %all-to-all-done = bf16[64,96,128]{2,1,0:T(8,128)(2,1)S(1)} async-done(((bf16[64,96,128]{2,1,0:T(8,128)(2,1)}), bf16[64,96,128]{2,1,0:T(8,128)(2,1)S(1)}, u32[]{:S(2)}, u32[]{:S(2)}) %all-to-all-start) | async-done | bytes 1572896 | tf_op jit(solution)/shard_map/all_to_all | solution.py:189
  37.9 1.4 %broadcast_in_dim.29 = bf16[64,96,128]{2,1,0:T(8,128)(2,1)} broadcast(bf16[96,128]{1,0:T(8,128)(2,1)S(1)} %dynamic-slice_bitcast_fusion), dimensions={1,2} | broadcast | bytes 1597440 | tf_op jit(solution)/shard_map/broadcast_in_dim | solution.py:195
  39.2 0.0 copy-start.2
  39.2 5.6 %all-to-all-start.1 = ((bf16[64,96,128]{2,1,0:T(8,128)(2,1)}), bf16[64,96,128]{2,1,0:T(8,128)(2,1)}, u32[]{:S(2)}, u32[]{:S(2)}) async-start(bf16[64,96,128]{2,1,0:T(8,128)(2,1)} %broadcast_in_dim.29), calls=%async_computation.1 | async-start | bytes 3145728 | tf_op jit(solution)/shard_map/all_to_all | solution.py:196
  44.9 0.0 copy-done.2
  44.9 0.1 iota_compare_fusion
  45.0 0.0 copy-done
  45.0 6.1 %fusion.8.rg_ref = bf16[2,256,768]{2,1,0:T(8,128)(2,1)S(1)} fusion(bf16[2,768,2880]{1,2,0:T(8,128)(2,1)} %param.7, bf16[2880,256]{1,0:T(8,128)(2,1)S(1)} %copy-done, pred[2,768]{1,0:T(4,128)(4,1)S(1)} %iota_compare_fusion), kind=kOutput, calls=%fused_computation.4 | convolution fusion | flops 2265710592 | bytes 11109888 | tf_op jit(solution)/shard_map/dot_general | solution.py:198
  51.1 15.6 %all-to-all-done.1 = bf16[64,96,128]{2,1,0:T(8,128)(2,1)} async-done(((bf16[64,96,128]{2,1,0:T(8,128)(2,1)}), bf16[64,96,128]{2,1,0:T(8,128)(2,1)}, u32[]{:S(2)}, u32[]{:S(2)}) %all-to-all-start.1) | async-done | bytes 1572896 | tf_op jit(solution)/shard_map/all_to_all | solution.py:196
  66.7 3.4 %collective-permute-start = (bf16[6144,128]{1,0:T(8,128)(2,1)}, bf16[6144,128]{1,0:T(8,128)(2,1)S(1)}, u32[]{:S(2)}, u32[]{:S(2)}) collective-permute-start(bf16[6144,128]{1,0:T(8,128)(2,1)} %bitcast.7.basis_ref), channel_id=1, source_target_pairs={{0,1},{1,0},{2,3},{3,2},{4,5},{5,4},{6,7},{7,6},{8,9},{9,8},{10,11... | collective-permute-start | bytes 4718600 | tf_op jit(solution)/shard_map/ppermute | solution.py:206
  70.1 6.4 %shard_map.65.first_ref = f32[2,768,512]{2,1,0:T(8,128)S(1)} custom-call(bf16[2,2,768,1440]{3,2,1,0:T(8,128)(2,1)} %shard_map.64.act_ref, bf16[6144,128]{1,0:T(8,128)(2,1)} %bitcast.7.basis_ref), custom_call_target="tpu_custom_call" | custom-call | flops 2264924160 | bytes 4423680 | tf_op jit(solution)/shard_map/pallas_call | solution.py:86
  76.5 0.0 collective-permute-done.basis_ref
  76.5 10.6 %shard_map.66 = (f32[2,128,512]{2,1,0:T(8,128)}, f32[2,128,512]{2,1,0:T(8,128)}, f32[128,8,128]{2,1,0:T(8,128)}) custom-call(s32[1]{0:T(128)} %bitcast.e_ref, bf16[2,2,768,1440]{3,2,1,0:T(8,128)(2,1)} %shard_map.64.act_ref, bf16[2,256,768]{2,1,0:T(8,128)(2,1)S(1)} %fusion.8.rg_ref, f32[2,768,512]{2,1,0:T(8,128)S(1)} %shard_map.65.first_ref, ...), custom_call_target="tpu_custom_call" | custom-call | flops 2264924160 | bytes 4423680 | tf_op jit(solution)/shard_map/pallas_call | solution.py:106
  87.1 0.0 copy-start.1
  87.1 3.7 %all-to-all-start.2 = ((f32[128,8,128]{2,1,0:T(8,128)}), f32[128,8,128]{2,1,0:T(8,128)S(1)}, u32[]{:S(2)}, u32[]{:S(2)}) async-start(f32[128,8,128]{2,1,0:T(8,128)} %get-tuple-element.16), calls=%async_computation.2 | async-start | bytes 1048576 | tf_op jit(solution)/shard_map/all_to_all | solution.py:210
  90.8 1.1 collective-permute-start.1
  92.0 12.6 %all-to-all-done.2 = f32[128,8,128]{2,1,0:T(8,128)S(1)} async-done(((f32[128,8,128]{2,1,0:T(8,128)}), f32[128,8,128]{2,1,0:T(8,128)S(1)}, u32[]{:S(2)}, u32[]{:S(2)}) %all-to-all-start.2) | async-done | bytes 524320 | tf_op jit(solution)/shard_map/all_to_all | solution.py:210
  104.5 0.1 reduce_sum.9
  104.7 0.8 broadcast_in_dim.32
  105.5 4.5 %all-to-all-start.3 = ((f32[128,8,128]{2,1,0:T(8,128)}), f32[128,8,128]{2,1,0:T(8,128)S(1)}, u32[]{:S(2)}, u32[]{:S(2)}) async-start(f32[128,8,128]{2,1,0:T(8,128)} %broadcast_in_dim.32), calls=%async_computation.3 | async-start | bytes 1048576 | tf_op jit(solution)/shard_map/all_to_all | solution.py:212
  110.1 0.0 collective-permute-done.1.got_ref
  110.1 13.7 %all-to-all-done.3.lam_ref = f32[128,8,128]{2,1,0:T(8,128)S(1)} async-done(((f32[128,8,128]{2,1,0:T(8,128)}), f32[128,8,128]{2,1,0:T(8,128)S(1)}, u32[]{:S(2)}, u32[]{:S(2)}) %all-to-all-start.3) | async-done | bytes 524320 | tf_op jit(solution)/shard_map/all_to_all | solution.py:212
  123.8 0.0 copy-done.1
  123.8 1.9 %shard_map.67 = f32[4,128,512]{2,1,0:T(8,128)} custom-call(s32[1]{0:T(128)} %bitcast.e_ref, f32[128,8,128]{2,1,0:T(8,128)S(1)} %all-to-all-done.3.lam_ref, f32[2,128,512]{2,1,0:T(8,128)S(1)} %copy-done.1, f32[2,128,512]{2,1,0:T(8,128)S(1)} %collective-permute-done.1.got_ref), custom_call_target="tpu_custom_call" | custom-call | tf_op jit(solution)/shard_map/pallas_call | solution.py:164
  (2 shorter events, 0.0 us)
Async XLA Ops:
  0.0 45.0 %copy-start = (bf16[2880,256]{1,0:T(8,128)(2,1)S(1)}, bf16[2880,256]{1,0:T(8,128)(2,1)}, u32[]{:S(2)}) copy-start(bf16[2880,256]{1,0:T(8,128)(2,1)} %param.8) | copy-start | bytes 4423684
  2.8 12.1 %copy-start.3 = (s32[4]{0:T(128)S(1)}, s32[4]{0:T(128)}, u32[]{:S(2)}) copy-start(s32[4]{0:T(128)} %param.10) | copy-start | bytes 52
  2.8 35.1 %all-to-all-start = ((bf16[64,96,128]{2,1,0:T(8,128)(2,1)}), bf16[64,96,128]{2,1,0:T(8,128)(2,1)S(1)}, u32[]{:S(2)}, u32[]{:S(2)}) async-start(bf16[64,96,128]{2,1,0:T(8,128)(2,1)} %pad.4), calls=%async_computation | async-start | bytes 3145728 | tf_op jit(solution)/shard_map/all_to_all | solution.py:189
  39.2 5.7 %copy-start.2 = (s32[2]{0:T(128)S(1)}, s32[2]{0:T(128)}, u32[]{:S(2)}) copy-start(s32[2]{0:T(128)} %param.11) | copy-start | bytes 28
  39.2 27.5 %all-to-all-start.1 = ((bf16[64,96,128]{2,1,0:T(8,128)(2,1)}), bf16[64,96,128]{2,1,0:T(8,128)(2,1)}, u32[]{:S(2)}, u32[]{:S(2)}) async-start(bf16[64,96,128]{2,1,0:T(8,128)(2,1)} %broadcast_in_dim.29), calls=%async_computation.1 | async-start | bytes 3145728 | tf_op jit(solution)/shard_map/all_to_all | solution.py:196
  66.7 9.8 %collective-permute-start = (bf16[6144,128]{1,0:T(8,128)(2,1)}, bf16[6144,128]{1,0:T(8,128)(2,1)S(1)}, u32[]{:S(2)}, u32[]{:S(2)}) collective-permute-start(bf16[6144,128]{1,0:T(8,128)(2,1)} %bitcast.7.basis_ref), channel_id=1, source_target_pairs={{0,1},{1,0},{2,3},{3,2},{4,5},{5,4},{6,7},{7,6},{8,9},{9,8},{10,11... | collective-permute-start | bytes 4718600 | tf_op jit(solution)/shard_map/ppermute | solution.py:206
  87.1 36.6 %copy-start.1 = (f32[2,128,512]{2,1,0:T(8,128)S(1)}, f32[2,128,512]{2,1,0:T(8,128)}, u32[]{:S(2)}) copy-start(f32[2,128,512]{2,1,0:T(8,128)} %get-tuple-element.17.keep_ref) | copy-start | bytes 1572868
  87.1 17.4 %all-to-all-start.2 = ((f32[128,8,128]{2,1,0:T(8,128)}), f32[128,8,128]{2,1,0:T(8,128)S(1)}, u32[]{:S(2)}, u32[]{:S(2)}) async-start(f32[128,8,128]{2,1,0:T(8,128)} %get-tuple-element.16), calls=%async_computation.2 | async-start | bytes 1048576 | tf_op jit(solution)/shard_map/all_to_all | solution.py:210
  90.8 19.2 %collective-permute-start.1 = (f32[2,128,512]{2,1,0:T(8,128)}, f32[2,128,512]{2,1,0:T(8,128)S(1)}, u32[]{:S(2)}, u32[]{:S(2)}) collective-permute-start(f32[2,128,512]{2,1,0:T(8,128)} %get-tuple-element.18), channel_id=1, source_target_pairs={{0,1},{1,0},{2,3},{3,2},{4,5},{5,4},{6,7},{7,6},{8,9},{9,8},{10,11... | collective-permute-start | bytes 1572872 | tf_op jit(solution)/shard_map/ppermute | solution.py:209
  105.5 18.2 %all-to-all-start.3 = ((f32[128,8,128]{2,1,0:T(8,128)}), f32[128,8,128]{2,1,0:T(8,128)S(1)}, u32[]{:S(2)}, u32[]{:S(2)}) async-start(f32[128,8,128]{2,1,0:T(8,128)} %broadcast_in_dim.32), calls=%async_computation.3 | async-start | bytes 1048576 | tf_op jit(solution)/shard_map/all_to_all | solution.py:212
